TPU v7x, 512 devices: a whole 4x8x8 slice. The times are simulated.
512 devices in a mesh: row: 16 (over z, y_lo), col: 8 (over y_hi, core), rep: 4 (over x).
Axes of the slice: x: 4, y: 8 (y_hi: 4, y_lo: 2; y = y_hi * 2 + y_lo), z: 8, core: 2. Of those that a mesh axis runs over, the one named last changes fastest.
Arguments:
- genotypes: bfloat16 [2048, 16384], P(('row', 'col', 'rep')), may hold values from 0 to 2, as said below
Outputs:
- main_tiles: float32 [16, 8, 1024, 1024], P('row', 'col', 'rep')
- half_tiles: float32 [16, 1024, 1024], P('row', 'rep', 'col')
Inputs may be any that keep to these rules, and one draw needn't show every extreme that they name: `genotypes`: imputed dosages of the alternate allele, real-valued.
All inputs are finite; a program needn't handle non-finite values.
Results may differ from a plain program's by a relative error of at most 0.008.
Values may be sent and summed in bfloat16 or wider, within the bound.
No kernel may reach another device: no remote copies, remote signals or barrier semaphores. Data moves between devices by JAX's collectives and lax.ppermute only.
A program may use at most 64 MiB of HBM per device.

v0:
```python
import jax
import jax.numpy as jnp
import numpy as np
from jax import lax
from jax.sharding import PartitionSpec as P


def copy_for_each(x, axis):
    copies = jnp.broadcast_to(x, (lax.axis_size(axis), *x.shape))
    return lax.all_to_all(copies, axis, split_axis=0, concat_axis=0, tiled=True)


def over_copies(x, axis):
    return copy_for_each(x, axis).sum(axis=0)


def packed_total(arrays, axis):
    ends = [0]
    for a in arrays:
        ends.append(ends[-1] + a.size)
    total = over_copies(jnp.concatenate([a.ravel() for a in arrays]), axis)
    return tuple((total[b:e].reshape(a.shape) for a, b, e in zip(arrays, ends, ends[1:])))


def cut_along(x, dim, length):
    before, after = (x.shape[:dim], x.shape[dim + 1 :])
    return jnp.moveaxis(x.reshape(*before, length, -1, *after), dim, 0)


def summed_on_arrival(x, axis, dim):
    length = lax.axis_size(axis)
    blocks = lax.all_to_all(cut_along(x, dim, length), axis, 0, 0, tiled=True)
    return jnp.sum(blocks.astype(jnp.float32), axis=0)


def body(genotypes):
    sample_rows, variants = genotypes.shape
    row_count = lax.axis_size("row")
    col_count = lax.axis_size("col")
    rep_count = lax.axis_size("rep")
    sample_count = sample_rows * row_count * col_count * rep_count
    block_width = variants // row_count
    slab_width = block_width // col_count
    pair_count = row_count * col_count
    blocked = genotypes.reshape(sample_rows, row_count, block_width)
    shift_table = np.array(
        [(brow + bcol) % row_count for brow in range(row_count) for bcol in range(col_count)],
        np.int32,
    )
    partner = jnp.take(blocked, shift_table, axis=1)
    slab_view = genotypes.reshape(sample_rows, pair_count, slab_width)
    far_slab = jnp.roll(slab_view, -(pair_count // 2), axis=1)
    own_block = jnp.broadcast_to(
        blocked[:, :, None, :], (sample_rows, row_count, col_count, block_width)
    )
    payload = jnp.concatenate(
        [partner, own_block.reshape(sample_rows, pair_count, block_width), far_slab], axis=2
    )
    payload_width = payload.shape[2]
    arrived = lax.all_to_all(payload, ("row", "col"), split_axis=1, concat_axis=0, tiled=True)
    arrived = arrived.reshape(-1, payload_width)
    values = arrived.astype(jnp.float32)
    col_dose, col_square = packed_total(
        (jnp.sum(values, axis=0), jnp.sum(values * values, axis=0)), "rep"
    )
    col_mean = col_dose / sample_count
    col_spread = col_square / sample_count - col_mean * col_mean
    arrived = ((values - col_mean) * lax.rsqrt(col_spread + 1e-05)).astype(jnp.bfloat16)
    scale_factor = 1.0 / sample_count
    right_side = jnp.concatenate(
        [arrived[:, :block_width], arrived[:, payload_width - slab_width :]], axis=1
    )
    product = lax.dot_general(
        arrived[:, block_width : 2 * block_width],
        right_side,
        (((0,), (0,)), ((), ())),
        preferred_element_type=jnp.float32,
    )
    partial_value = product * scale_factor
    summed = summed_on_arrival(partial_value.astype(jnp.bfloat16), "rep", 0)
    main_tile = summed[:, :block_width].reshape(1, 1, -1, block_width)
    half_tile = summed[:, block_width:].reshape(1, -1, slab_width)
    return (main_tile, half_tile)


def solution(mesh):
    placed = (P(("row", "col", "rep"), None),)
    return jax.shard_map(
        body,
        mesh=mesh,
        in_specs=placed,
        out_specs=(P("row", "col", "rep", None), P("row", "rep", "col")),
        check_vma=False,
    )
```

profile of v0, /device:TPU:1, one launch (start us, length us, event | category | flops | bytes accessed | tf_op | source)
XLA Modules:
  0.0 138.2 jit_solution(16736934565368421999)
XLA Ops:
  0.6 0.0 copy-start
  0.6 0.7 pad_clamp_fusion
  1.3 0.9 fusion.10
  2.3 2.4 %gather_fusion = bf16[128,4,1024]{2,1,0:T(4,128)(2,1)S(1)} fusion(bf16[4,16,1024]{2,0,1:T(4,128)(2,1)} %bitcast.16, s32[1024]{0:T(1024)S(1)} %pad_clamp_fusion), kind=kCustom, calls=%fused_computation | custom fusion | bytes 2097664 | tf_op jit(solution)/shard_map/jit(_take)/gather | solution.py:50
  4.6 0.0 copy-done
  4.6 0.3 broadcast_in_dim.25
  4.9 5.4 %maximum_maximum_fusion = bf16[4,128,2176]{2,0,1:T(4,128)(2,1)S(1)} fusion(bf16[4,64,128]{2,0,1:T(4,128)(2,1)S(1)} %get-tuple-element.5, bf16[4,64,128]{2,0,1:T(4,128)(2,1)S(1)} %get-tuple-element.4, bf16[4,128,1024]{2,0,1:T(4,128)(2,1)S(1)} %bitcast.19, bf16[4,128,1024]{2,0,1:T(4,128)(2,1)S(1)} %bitcast.18), kind=kLoop, calls=%fused_computation.9 | loop fusion | flops 8912896 | bytes 4456448 | tf_op jit(solution)/shard_map/concatenate | solution.py:56
  10.4 74.3 %all_to_all.20 = bf16[4,128,2176]{2,0,1:T(4,128)(2,1)S(1)} all-to-all(bf16[4,128,2176]{2,0,1:T(4,128)(2,1)S(1)} %maximum_maximum_fusion), channel_id=1, replica_groups=mesh['row'=16,'col'=8,'rep'=4] {'row','col'}, dimensions={1} | all-to-all | bytes 4456448 | tf_op jit(solution)/shard_map/all_to_all | solution.py:60
  84.7 1.8 %convert_reduce_fusion = (f32[2176]{0:T(1024)S(1)}, f32[2176]{0:T(1024)S(1)}) fusion(bf16[4,128,2176]{2,0,1:T(4,128)(2,1)S(1)} %all_to_all.20), kind=kLoop, calls=%fused_computation.2 | loop fusion | flops 4452096 | bytes 2245632 | tf_op jit(solution)/shard_map/reduce_sum | solution.py:64
  86.4 0.7 broadcast_in_dim.26
  87.1 4.0 %all-to-all-start.1 = ((f32[4,1,4352]{2,1,0:T(1,128)}), f32[4,1,4352]{2,1,0:T(1,128)S(1)}, u32[]{:S(2)}, u32[]{:S(2)}) async-start(f32[4,1,4352]{2,1,0:T(1,128)} %broadcast_in_dim.26), calls=%async_computation.1 | async-start | bytes 139264 | tf_op jit(solution)/shard_map/all_to_all | solution.py:10
  91.1 2.6 %convert_bitcast_fusion = f32[128,4,1,2176]{3,1,0,2:T(4,128)} fusion(bf16[4,128,2176]{2,0,1:T(4,128)(2,1)S(1)} %all_to_all.20), kind=kLoop, calls=%fused_computation.3 | loop fusion | flops 1114112 | bytes 6684672 | tf_op jit(solution)/shard_map/convert_element_type | solution.py:62
  93.7 5.6 %reshape.48 = f32[512,2176]{1,0:T(8,128)} reshape(f32[128,4,1,2176]{3,1,0,2:T(4,128)} %convert_bitcast_fusion) | data formatting | bytes 8912896 | tf_op jit(solution)/shard_map/convert_element_type | solution.py:62
  99.3 0.0 all-to-all-done.1
  99.3 0.1 reduce_sum.38
  99.4 2.7 %multiply_convert_fusion = bf16[512,2176]{1,0:T(8,128)(2,1)S(1)} fusion(f32[512,2176]{1,0:T(8,128)} %reshape.48, f32[2176]{0:T(1024)S(1)} %get-tuple-element.7, f32[2176]{0:T(1024)S(1)} %get-tuple-element.6), kind=kLoop, calls=%fused_computation.7 | loop fusion | flops 3342336 | bytes 6702080 | tf_op jit(solution)/shard_map/convert_element_type | solution.py:68
  102.1 0.1 slice.45
  102.2 1.6 %fusion.1 = bf16[1024,1152]{1,0:T(8,128)(2,1)S(1)} fusion(bf16[512,128]{1,0:T(8,128)(2,1)S(1)} %slice.46, bf16[512,1024]{1,0:T(8,128)(2,1)S(1)} %slice.45, bf16[512,2176]{1,0:T(8,128)(2,1)S(1)} %multiply_convert_fusion), kind=kOutput, calls=%fused_computation.8 | convolution fusion | flops 1212678144 | bytes 4587520 | tf_op jit(solution)/shard_map/dot_general | solution.py:73
  103.8 32.3 %all_to_all.21 = bf16[4,256,1152]{2,1,0:T(8,128)(2,1)S(1)} all-to-all(bf16[4,256,1152]{2,1,0:T(8,128)(2,1)S(1)} %bitcast.20), channel_id=1, replica_groups=mesh['row'=16,'col'=8,'rep'=4] {'rep'}, dimensions={0} | all-to-all | bytes 4718592 | tf_op jit(solution)/shard_map/all_to_all | solution.py:32
  136.1 0.3 convert_reduce_fusion.1
  136.5 0.7 slice_bitcast_fusion.1
  137.1 1.1 slice_bitcast_fusion
  (3 shorter events, 0.0 us)
Async XLA Ops:
  0.6 4.0 %copy-start = (bf16[4,16384]{1,0:T(4,128)(2,1)S(1)}, bf16[4,16384]{1,0:T(4,128)(2,1)}, u32[]{:S(2)}) copy-start(bf16[4,16384]{1,0:T(4,128)(2,1)} %param.2) | copy-start | bytes 393220
  87.1 12.2 %all-to-all-start.1 = ((f32[4,1,4352]{2,1,0:T(1,128)}), f32[4,1,4352]{2,1,0:T(1,128)S(1)}, u32[]{:S(2)}, u32[]{:S(2)}) async-start(f32[4,1,4352]{2,1,0:T(1,128)} %broadcast_in_dim.26), calls=%async_computation.1 | async-start | bytes 139264 | tf_op jit(solution)/shard_map/all_to_all | solution.py:10
where the time goes:
time: 139 us; the launch traced here: 138 us
  blocking collectives  107 us (77%)
  other arithmetic  13.6 us (10%)
  local copies, waits for them, and re-layouts  11.7 us (8%)
  starting transfers between devices  4.01 us (3%)
  matrix products  1.59 us (1%)
    all_to_all x1, blocking collectives, body(): lax.all_to_all(payload, ('row', 'col'), split_axis=1, concat_axis=0, tile...  74.3 us
    all_to_all x1, blocking collectives, summed_on_arrival(): blocks = lax.all_to_all(cut_along(x, dim, length), axis, 0, 0, tiled=True)  32.3 us
    convert_element_type x1, local copies, waits for them, and re-layouts, body(): values = arrived.astype(jnp.float32)  5.55 us
    concatenate x1, other arithmetic, body(): jnp.concatenate([partner, own_block.reshape(sample_rows, pair_count, bloc...  5.44 us
    all_to_all x1, starting transfers between devices, copy_for_each(): return lax.all_to_all(copies, axis, split_axis=0, concat_axis=0, tiled=True)  4.01 us
  transfers between devices with their start and end apart: 1, of which 0 were waited for; matrix products, arithmetic and copies ran while one was open for 6% of the time, Pallas kernels for 0%

commit v1 on v0

v1 whole, which is shorter than its diff:
```python
import functools

import jax
import jax.numpy as jnp
from jax import lax
from jax.experimental import pallas as pl
from jax.experimental.pallas import tpu as pltpu
from jax.sharding import PartitionSpec as P

F32 = jnp.float32
BF16 = jnp.bfloat16
EPS = 1e-05


def thirds(v):
    hi = v.astype(BF16).astype(F32)
    rest = v - hi
    mid = rest.astype(BF16).astype(F32)
    return hi, mid, (rest - mid).astype(BF16).astype(F32)


def pack_body(n_row, n_col, x_ref, out_ref):
    width = x_ref.shape[1] // n_row
    half, slab = width // 2, width // n_col
    for r in range(n_row):
        for c in range(n_col):
            d = r * n_col + c
            near = r * width + (c % 2) * half
            pair = ((r + c) % n_row) * width
            far = ((r + n_row // 2) % n_row) * width + c * slab
            out_ref[d, :, :half] = x_ref[:, near : near + half]
            out_ref[d, :, half : half + width] = x_ref[:, pair : pair + width]
            out_ref[d, :, half + width :] = x_ref[:, far : far + slab]


def sums(v):
    v = v.astype(F32)
    return jnp.sum(v, axis=0, keepdims=True), jnp.sum(v * v, axis=0, keepdims=True)


def tile_body(n_rep, own_ref, other_ref, out_ref):
    samples, half = other_ref.shape
    sub = 2 * half // n_rep
    core = lax.rem(lax.axis_index("col"), 2)
    right = own_ref[:, half:]
    cols = right.shape[1]
    dose, square = sums(right)
    hi, mid, lo = thirds(dose)
    fold = -1.0 / samples
    pad = jnp.zeros((2, cols), F32)
    right_fix = (jnp.concatenate([hi, mid, hi, mid, lo, hi, pad], axis=0) * fold).astype(BF16)
    mean = dose / samples
    col_rows = [*thirds(mean), *thirds(square - dose * mean)]
    per_half = n_rep // 2
    for side, ref in enumerate((own_ref, other_ref)):
        for j in range(per_half):
            left = ref[:, j * sub : (j + 1) * sub]
            l_dose, l_square = sums(left)
            hi, mid, lo = thirds(l_dose)
            pad = jnp.zeros((2, sub), F32)
            left_fix = jnp.concatenate([hi, hi, mid, mid, hi, lo, pad], axis=0).astype(BF16)
            part = lax.dot_general(left, right, (((0,), (0,)), ((), ())), preferred_element_type=F32)
            part += lax.dot_general(left_fix, right_fix, (((0,), (0,)), ((), ())), preferred_element_type=F32)
            l_mean = l_dose / samples
            gap = jnp.zeros((1, cols - 3 * sub), F32)
            rows = [
                jnp.concatenate([*thirds(l_mean), gap], axis=1),
                jnp.concatenate([*thirds(l_square - l_dose * l_mean), gap], axis=1),
            ]
            to = lax.rem(per_half * (side + core), n_rep) + j
            out_ref[to, :sub, :] = part.astype(BF16)
            out_ref[to, sub:, :] = jnp.concatenate(col_rows + rows, axis=0).astype(BF16)


def whole(means, squares, samples):
    count = len(means)
    mean = sum(means) / count
    off = [m - mean for m in means]
    spread = sum(squares) / (count * samples) + sum(o * o for o in off) / count
    return off, lax.rsqrt(spread + EPS)


def join_body(samples, in_ref, main_ref, half_ref):
    n_rep, rows, cols = in_ref.shape
    sub = rows - 8
    width = main_ref.shape[1]
    total = sum(in_ref[q, :sub, :].astype(F32) for q in range(n_rep))
    stats = [in_ref[q, sub:, :].astype(F32) for q in range(n_rep)]
    three = lambda s, i: s[i : i + 1] + s[i + 1 : i + 2] + s[i + 2 : i + 3]
    flat = lambda s, i: s[i : i + 1, :sub] + s[i : i + 1, sub : 2 * sub] + s[i : i + 1, 2 * sub : 3 * sub]
    off, scale = whole([three(s, 0) for s in stats], [three(s, 3) for s in stats], samples)
    l_off, l_scale = whole([flat(s, 6) for s in stats], [flat(s, 7) for s in stats], samples)
    pad = [jnp.zeros((1, sub), F32)] * (7 - n_rep)
    turned = jnp.concatenate(l_off + [l_scale / (n_rep * samples)] + pad, axis=0).T
    for q in range(n_rep):
        total += (turned[:, q : q + 1] * samples) * off[q]
    total = total * turned[:, n_rep : n_rep + 1] * scale
    main_ref[...] = total[:, :width]
    half_ref[...] = total[:, width:]


def body(genotypes):
    sample_rows, variants = genotypes.shape
    n_row, n_col, n_rep = (lax.axis_size(a) for a in ("row", "col", "rep"))
    width = variants // n_row
    half, slab = width // 2, width // n_col
    pairs = n_row * n_col
    samples = sample_rows * pairs
    wide = half + width + slab
    cols = width + slab
    sub = width // n_rep
    payload = pl.pallas_call(
        functools.partial(pack_body, n_row, n_col),
        out_shape=jax.ShapeDtypeStruct((pairs, sample_rows, wide), BF16),
        name="pack",
    )(genotypes)
    arrived = lax.all_to_all(payload, ("row", "col"), 0, 0, tiled=True)
    swap = [(c, c ^ 1) for c in range(n_col)]
    other = lax.ppermute(arrived[:, :, :half], "col", swap)
    partial = pl.pallas_call(
        functools.partial(tile_body, n_rep),
        out_shape=jax.ShapeDtypeStruct((n_rep, sub + 8, cols), BF16),
        name="tile",
    )(arrived.reshape(samples, wide), other.reshape(samples, half))
    parts = lax.all_to_all(partial, "rep", 0, 0, tiled=True)
    main, far = pl.pallas_call(
        functools.partial(join_body, samples),
        out_shape=(jax.ShapeDtypeStruct((sub, width), F32), jax.ShapeDtypeStruct((sub, slab), F32)),
        name="join",
    )(parts)
    return main.reshape(1, 1, sub, width), far.reshape(1, sub, slab)


def solution(mesh):
    return jax.shard_map(
        body,
        mesh=mesh,
        in_specs=(P(("row", "col", "rep"), None),),
        out_specs=(P("row", "col", "rep", None), P("row", "rep", "col")),
        check_vma=False,
    )
```

time: 139 us -> 115 us (0.83)
  other arithmetic: 13.6 us -> 0 us
  Pallas kernels: 0 us -> 11.2 us
  local copies, waits for them, and re-layouts: 11.7 us -> 2.49 us
  blocking collectives: 107 us -> 97.8 us
  starting transfers between devices: 4.01 us -> 1.92 us
  matrix products: 1.59 us -> 0 us
    pallas_call x0 -> x3, Pallas kernels: none -> 11.2 us  [the longest x1 5.33 us: body(): pl.pallas_call(functools.partial(tile_body, n_rep), out_shape=jax.ShapeDt...]
    all_to_all x2, blocking collectives: 107 us -> 97.8 us  [the longest x1 63.4 us: body(): arrived = lax.all_to_all(payload, ('row', 'col'), 0, 0, tiled=True)]
    convert_element_type x1 -> x0, local copies, waits for them, and re-layouts: 5.55 us -> none  [body(): values = arrived.astype(jnp.float32)]
    concatenate x2 -> x0, other arithmetic: 5.45 us -> none  [the longest x1 5.44 us: body(): jnp.concatenate([partner, own_block.reshape(sample_rows, pair_count, bloc...]
    convert_element_type x2 -> x0, other arithmetic: 5.27 us -> none  [the longest x1 2.66 us: body(): ((values - col_mean) * lax.rsqrt(col_spread + 1e-05)).astype(jnp.bfloat16)]
    all_to_all x1 -> x0, starting transfers between devices: 4.01 us -> none  [copy_for_each(): return lax.all_to_all(copies, axis, split_axis=0, concat_axis=0, tiled=True)]
    gather x1 -> x0, local copies, waits for them, and re-layouts: 2.35 us -> none  [body(): partner = jnp.take(blocked, shift_table, axis=1)]
    reduce_sum x3 -> x0, other arithmetic: 2.18 us -> none  [the longest x1 1.76 us: body(): jnp.sum(values, axis=0)]
  transfers between devices with their start and end apart: 1 -> 1, of which waited for: 0 -> 1; matrix products, arithmetic and copies ran while one was open for 6% -> 1% of each run, Pallas kernels for 0% -> 0%
where the time goes in v1:
time: 115 us
  blocking collectives  97.8 us (85%)
  Pallas kernels  11.2 us (10%)
  local copies, waits for them, and re-layouts  2.49 us (2%)
  starting transfers between devices  1.92 us (2%)
    all_to_all x1, blocking collectives, body(): arrived = lax.all_to_all(payload, ('row', 'col'), 0, 0, tiled=True)  63.4 us
    all_to_all x1, blocking collectives, body(): parts = lax.all_to_all(partial, 'rep', 0, 0, tiled=True)  34.4 us
    pallas_call x1, Pallas kernels, body(): pl.pallas_call(functools.partial(tile_body, n_rep), out_shape=jax.ShapeDt...  5.33 us
    pallas_call x1, Pallas kernels, body(): pl.pallas_call(functools.partial(join_body, samples), out_shape=(jax.Shap...  3.62 us
  transfers between devices with their start and end apart: 1, of which 1 were waited for; matrix products, arithmetic and copies ran while one was open for 1% of the time, Pallas kernels for 0%

profile of v1, /device:TPU:1, one launch (start us, length us, event | category | flops | bytes accessed | tf_op | source)
XLA Modules:
  0.0 114.5 jit_solution(6009550229497143450)
XLA Ops:
  0.6 2.2 %pack.1 = bf16[128,4,1664]{2,1,0:T(4,128)(2,1)} custom-call(bf16[4,16384]{1,0:T(4,128)(2,1)} %x_ref.1), custom_call_target="tpu_custom_call" | custom-call | tf_op jit(solution)/shard_map/pack/pallas_call | solution.py:112
  2.9 63.4 %all_to_all.10 = bf16[128,4,1664]{2,1,0:T(4,128)(2,1)S(1)} all-to-all(bf16[128,4,1664]{2,1,0:T(4,128)(2,1)} %pack.1), channel_id=1, replica_groups=mesh['row'=16,'col'=8,'rep'=4] {'row','col'}, dimensions={0} | all-to-all | bytes 3407872 | tf_op jit(solution)/shard_map/all_to_all | solution.py:117
  66.3 0.2 slice.4
  66.5 1.9 %collective-permute-start = (bf16[128,4,512]{2,1,0:T(4,128)(2,1)S(1)}, bf16[128,4,512]{2,1,0:T(4,128)(2,1)S(1)}, u32[]{:S(2)}, u32[]{:S(2)}) collective-permute-start(bf16[128,4,512]{2,1,0:T(4,128)(2,1)S(1)} %slice.4), channel_id=1, source_target_pairs={{0,4},{4,0},{8,12},{12,8},{16,20},{20,16},{24,28},{28,24},{1,5},{5... | collective-permute-start | bytes 1572872 | tf_op jit(solution)/shard_map/ppermute | solution.py:119
  68.4 1.4 %reshape.16.own_ref = bf16[512,1664]{1,0:T(8,128)(2,1)} reshape(bf16[128,4,1664]{2,1,0:T(4,128)(2,1)S(1)} %all_to_all.10) | data formatting | bytes 3407872 | tf_op jit(solution)/shard_map/reshape | solution.py:124
  69.8 0.5 collective-permute-done
  70.3 0.9 reshape.17.other_ref
  71.2 5.3 %tile.1 = bf16[4,264,1152]{2,1,0:T(8,128)(2,1)} custom-call(bf16[512,1664]{1,0:T(8,128)(2,1)} %reshape.16.own_ref, bf16[512,512]{1,0:T(8,128)(2,1)} %reshape.17.other_ref), custom_call_target="tpu_custom_call" | custom-call | tf_op jit(solution)/shard_map/tile/pallas_call | solution.py:120
  76.5 34.4 %all_to_all.11.in_ref = bf16[4,264,1152]{2,1,0:T(8,128)(2,1)} all-to-all(bf16[4,264,1152]{2,1,0:T(8,128)(2,1)} %tile.1), channel_id=1, replica_groups=mesh['row'=16,'col'=8,'rep'=4] {'rep'}, dimensions={0} | all-to-all | bytes 4866048 | tf_op jit(solution)/shard_map/all_to_all | solution.py:125
  110.9 3.6 %join.1 = (f32[256,1024]{1,0:T(8,128)}, f32[256,128]{1,0:T(8,128)}) custom-call(bf16[4,264,1152]{2,1,0:T(8,128)(2,1)} %all_to_all.11.in_ref), custom_call_target="tpu_custom_call" | custom-call | tf_op jit(solution)/shard_map/join/pallas_call | solution.py:126
Async XLA Ops:
  66.5 3.8 %collective-permute-start = (bf16[128,4,512]{2,1,0:T(4,128)(2,1)S(1)}, bf16[128,4,512]{2,1,0:T(4,128)(2,1)S(1)}, u32[]{:S(2)}, u32[]{:S(2)}) collective-permute-start(bf16[128,4,512]{2,1,0:T(4,128)(2,1)S(1)} %slice.4), channel_id=1, source_target_pairs={{0,4},{4,0},{8,12},{12,8},{16,20},{20,16},{24,28},{28,24},{1,5},{5... | collective-permute-start | bytes 1572872 | tf_op jit(solution)/shard_map/ppermute | solution.py:119

commit v2 on v1

v2 whole, which is shorter than its diff:
```python
import functools

import jax
import jax.numpy as jnp
from jax import lax
from jax.experimental import pallas as pl
from jax.experimental.pallas import tpu as pltpu
from jax.sharding import PartitionSpec as P


F32 = jnp.float32
BF16 = jnp.bfloat16
EPS = 1e-05


def params(mib):
    return pltpu.CompilerParams(vmem_limit_bytes=mib << 20)


def cost(flops, size):
    return pl.CostEstimate(flops=flops, bytes_accessed=size, transcendentals=0)


def thirds(v):
    hi = v.astype(BF16).astype(F32)
    rest = v - hi
    mid = rest.astype(BF16).astype(F32)
    return hi, mid, (rest - mid).astype(BF16).astype(F32)


def sums(v):
    v = v.astype(F32)
    return jnp.sum(v, axis=0, keepdims=True), jnp.sum(v * v, axis=0, keepdims=True)


def stacked(rows, count):
    gap = jnp.zeros((count - len(rows), rows[0].shape[1]), F32)
    return jnp.concatenate([*rows, gap], axis=0)


def dot0(a, b):
    return lax.dot_general(a, b, (((0,), (0,)), ((), ())), preferred_element_type=F32)


def pack_first(n_row, n_col, x_ref, out_ref):
    width = x_ref.shape[1] // n_row
    half, slab = width // 2, width // n_col
    for r in range(n_row):
        for c in range(n_col):
            d = r * n_col + c
            near = r * width + (c % 2) * half
            pair = ((r + c) % n_row) * width
            far = ((r + n_row // 2) % n_row) * width + c * slab
            out_ref[d, :, :half] = x_ref[:, near : near + half]
            out_ref[d, :, half : 2 * half] = x_ref[:, pair : pair + half]
            out_ref[d, :, 2 * half :] = x_ref[:, far : far + slab]


def pack_second(n_row, n_col, x_ref, out_ref):
    width = x_ref.shape[1] // n_row
    half = width // 2
    for r in range(n_row):
        for c in range(n_col):
            pair = ((r + c) % n_row) * width + half
            out_ref[r * n_col + c] = x_ref[:, pair : pair + half]


def column_side(right):
    samples = right.shape[0]
    dose, square = sums(right)
    hi, mid, lo = thirds(dose)
    fix = (stacked([hi, mid, hi, mid, lo, hi], 8) * (-1.0 / samples)).astype(BF16)
    mean = dose / samples
    return fix, [*thirds(mean), *thirds(square - dose * mean)]


def tile_first(n_rep, own_ref, other_ref, left_ref, fix_ref, *out_refs):
    samples, half = other_ref.shape
    sub = 2 * half // n_rep
    core = lax.rem(lax.axis_index("col"), 2)
    group = lax.axis_index("rep")
    left_ref[:, pl.ds(pl.multiple_of(core * half, half), half)] = own_ref[:, :half]
    left_ref[:, pl.ds(pl.multiple_of((1 - core) * half, half), half)] = other_ref[...]
    right = own_ref[:, half:]
    cols = right.shape[1]
    right_fix, col_rows = column_side(right)
    gap = jnp.zeros((1, cols - sub), F32)
    for k in range(n_rep):
        at = pl.ds(pl.multiple_of(lax.rem(group + k, n_rep) * sub, sub), sub)
        left = left_ref[:, at]
        dose, square = sums(left)
        hi, mid, lo = thirds(dose)
        left_fix = stacked([hi, hi, mid, mid, hi, lo], 8).astype(BF16)
        fix_ref[:, at] = left_fix
        mean = dose / samples
        rows = [*thirds(mean), *thirds(square - dose * mean)]
        rows = [jnp.concatenate([v, gap], axis=1) for v in rows]
        part = dot0(left, right) + dot0(left_fix, right_fix)
        out_refs[k][:sub, :] = part.astype(BF16)
        out_refs[k][sub:, :] = stacked(col_rows + rows, 16).astype(BF16)


def tile_second(left_ref, fix_ref, right_ref, out_ref):
    n_rep, rows, _ = out_ref.shape
    sub = rows - 8
    right = right_ref[...]
    right_fix, col_rows = column_side(right)
    foot = stacked(col_rows, 8).astype(BF16)
    for q in range(n_rep):
        at = slice(q * sub, (q + 1) * sub)
        part = dot0(left_ref[:, at], right) + dot0(fix_ref[:, at], right_fix)
        out_ref[q, :sub, :] = part.astype(BF16)
        out_ref[q, sub:, :] = foot


def whole(means, squares, samples):
    count = len(means)
    mean = sum(means) / count
    off = [m - mean for m in means]
    spread = sum(squares) / (count * samples) + sum(o * o for o in off) / count
    return off, lax.rsqrt(spread + EPS)


def three(s, i):
    return s[i : i + 1] + s[i + 1 : i + 2] + s[i + 2 : i + 3]


def joined(parts, stats, turned, samples):
    n_rep = len(parts)
    off, scale = whole([three(s, 0) for s in stats], [three(s, 3) for s in stats], samples)
    total = sum(p.astype(F32) for p in parts)
    for q in range(n_rep):
        total += (turned[:, q : q + 1] * samples) * off[q]
    return total * turned[:, n_rep : n_rep + 1] * scale


def join_first(samples, *refs):
    *in_refs, turned_ref, main_ref, half_ref = refs
    n_rep = len(in_refs)
    sub, width = main_ref.shape
    stats = [r[sub:, :].astype(F32) for r in in_refs]
    l_off, l_scale = whole(
        [three(s[:, :sub], 6) for s in stats], [three(s[:, :sub], 9) for s in stats], samples
    )
    turned = stacked(l_off + [l_scale / (n_rep * samples)], 8).T
    total = joined([r[:sub, :] for r in in_refs], stats, turned, samples)
    main_ref[...] = total[:, :width]
    half_ref[...] = total[:, width:]
    group = lax.axis_index("rep")
    line = lax.broadcasted_iota(jnp.int32, (8, sub), 0)
    ordered = jnp.where(line == n_rep, l_scale / (n_rep * samples), 0.0)
    for k in range(n_rep):
        source = lax.rem(group + n_rep - k, n_rep)
        ordered = jnp.where(line == source, l_off[k], ordered)
    turned_ref[...] = ordered.T


def join_second(samples, in_ref, turned_ref, main_in, main_ref):
    n_rep, rows, _ = in_ref.shape
    sub = rows - 8
    stats = [in_ref[q, sub:, :].astype(F32) for q in range(n_rep)]
    parts = [in_ref[q, :sub, :] for q in range(n_rep)]
    main_ref[...] = joined(parts, stats, turned_ref[...], samples)


def steps(genotypes):
    sample_rows, variants = genotypes.shape
    n_row, n_col, n_rep = (lax.axis_size(a) for a in ("row", "col", "rep"))
    width = variants // n_row
    half, slab = width // 2, width // n_col
    pairs = n_row * n_col
    samples = sample_rows * pairs
    cols = half + slab
    sub = width // n_rep
    shape = jax.ShapeDtypeStruct

    def pack(fn, wide):
        return pl.pallas_call(
            functools.partial(fn, n_row, n_col),
            out_shape=shape((pairs, sample_rows, wide), BF16),
            compiler_params=params(8),
            cost_estimate=cost(0, 4 * pairs * sample_rows * wide),
        )(genotypes)

    send_first = pack(pack_first, half + cols)
    send_second = pack(pack_second, half)
    first = lax.all_to_all(send_first, ("row", "col"), 0, 0, tiled=True)
    second = lax.all_to_all(send_second, ("row", "col"), 0, 0, tiled=True)
    swap = [(c, c ^ 1) for c in range(n_col)]
    other = lax.ppermute(first[:, :, :half], "col", swap)
    left, fix, *parts = pl.pallas_call(
        functools.partial(tile_first, n_rep),
        out_shape=(
            shape((samples, width), BF16),
            shape((8, width), BF16),
            *[shape((sub + 16, cols), BF16)] * n_rep,
        ),
        compiler_params=params(16),
        cost_estimate=cost(2 * samples * width * cols, 2 * samples * (2 * width + cols)),
        name="tile_first",
    )(first.reshape(samples, half + cols), other.reshape(samples, half))
    for k in range(1, n_rep):
        parts[k] = lax.ppermute(parts[k], "rep", [(q, (q + k) % n_rep) for q in range(n_rep)])
    turned, main, far = pl.pallas_call(
        functools.partial(join_first, samples),
        grid=(1,),
        in_specs=[pl.BlockSpec((sub + 16, cols), lambda i: (0, 0))] * n_rep,
        out_specs=(
            pl.BlockSpec((sub, 8), lambda i: (0, 0)),
            pl.BlockSpec((sub, half), lambda i: (0, 0)),
            pl.BlockSpec((sub, slab), lambda i: (0, 0)),
        ),
        out_shape=(shape((sub, 8), F32), shape((sub, width), F32), shape((sub, slab), F32)),
        compiler_params=params(8),
        cost_estimate=cost(12 * sub * cols, 12 * sub * cols),
        name="join_first",
    )(*parts)
    partial = pl.pallas_call(
        tile_second,
        out_shape=shape((n_rep, sub + 8, half), BF16),
        compiler_params=params(16),
        cost_estimate=cost(2 * samples * width * half, 2 * samples * (width + half)),
        name="tile_second",
    )(left, fix, second.reshape(samples, half))
    rest = lax.all_to_all(partial, "rep", 0, 0, tiled=True)
    main = pl.pallas_call(
        functools.partial(join_second, samples),
        grid=(1,),
        in_specs=[
            pl.BlockSpec((n_rep, sub + 8, half), lambda i: (0, 0, 0)),
            pl.BlockSpec((sub, 8), lambda i: (0, 0)),
            pl.BlockSpec(memory_space=pl.ANY),
        ],
        out_specs=pl.BlockSpec((sub, half), lambda i: (0, 1)),
        out_shape=shape((sub, width), F32),
        input_output_aliases={2: 0},
        compiler_params=params(8),
        cost_estimate=cost(12 * sub * half, 12 * sub * half),
        name="join_second",
    )(rest, turned, main)
    return main.reshape(1, 1, sub, width), far.reshape(1, sub, slab)


def solution(mesh):
    return jax.shard_map(
        steps,
        mesh=mesh,
        in_specs=(P(("row", "col", "rep"), None),),
        out_specs=(P("row", "col", "rep", None), P("row", "rep", "col")),
        check_vma=False,
    )
```

time: 115 us -> 124 us (1.078)
  blocking collectives: 97.8 us -> 0 us
  waiting for transfers between devices: 0.49 us -> 69.4 us
  starting transfers between devices: 1.92 us -> 42.1 us
  Pallas kernels: 11.2 us -> 8.24 us
    all_to_all x2 -> x0, blocking collectives: 97.8 us -> none  [the longest x1 63.4 us: body(): arrived = lax.all_to_all(payload, ('row', 'col'), 0, 0, tiled=True)]
    all_to_all x0 -> x3, waiting for transfers between devices: none -> 49.7 us  [the longest x1 33.2 us: steps(): first = lax.all_to_all(send_first, ('row', 'col'), 0, 0, tiled=True)]
    all_to_all x0 -> x3, starting transfers between devices: none -> 28.6 us  [the longest x1 18.5 us: steps(): first = lax.all_to_all(send_first, ('row', 'col'), 0, 0, tiled=True)]
    ppermute x1 -> x4, waiting for transfers between devices: 0.49 us -> 19.7 us  [the longest x3 19.7 us: steps(): lax.ppermute(parts[k], 'rep', [(q, (q + k) % n_rep) for q in range(n_rep)])]
    ppermute x1 -> x4, starting transfers between devices: 1.92 us -> 13.5 us  [the longest x3 10.8 us: steps(): lax.ppermute(parts[k], 'rep', [(q, (q + k) % n_rep) for q in range(n_rep)])]
    pallas_call x3 -> x6, Pallas kernels: 11.2 us -> 8.24 us  [the longest x1 2.08 us: steps(): pl.pallas_call(tile_second, out_shape=shape((n_rep, sub + 8, half), BF16)...]
    reshape x2 -> x3, local copies, waits for them, and re-layouts: 2.3 us -> 0.56 us  [the longest x1 0.31 us: steps(): first.reshape(samples, half + cols)]
    unnamed x0 -> x8, local copies, waits for them, and re-layouts: none -> 1.63 us
  transfers between devices with their start and end apart: 1 -> 7, of which waited for: 1 -> 4; matrix products, arithmetic and copies ran while one was open for 1% -> 1% of each run, Pallas kernels for 0% -> 2%
where the time goes in v2:
time: 124 us
  waiting for transfers between devices  69.4 us (56%)
  starting transfers between devices  42.1 us (34%)
  Pallas kernels  8.24 us (7%)
  local copies, waits for them, and re-layouts  3.16 us (3%)
    all_to_all x1, waiting for transfers between devices, steps(): first = lax.all_to_all(send_first, ('row', 'col'), 0, 0, tiled=True)  33.2 us
    ppermute x3, waiting for transfers between devices, steps(): lax.ppermute(parts[k], 'rep', [(q, (q + k) % n_rep) for q in range(n_rep)])  19.7 us
    all_to_all x1, starting transfers between devices, steps(): first = lax.all_to_all(send_first, ('row', 'col'), 0, 0, tiled=True)  18.5 us
    all_to_all x1, waiting for transfers between devices, steps(): second = lax.all_to_all(send_second, ('row', 'col'), 0, 0, tiled=True)  16.5 us
    ppermute x3, starting transfers between devices, steps(): lax.ppermute(parts[k], 'rep', [(q, (q + k) % n_rep) for q in range(n_rep)])  10.8 us
    all_to_all x1, starting transfers between devices, steps(): second = lax.all_to_all(send_second, ('row', 'col'), 0, 0, tiled=True)  5.92 us
    all_to_all x1, starting transfers between devices, steps(): rest = lax.all_to_all(partial, 'rep', 0, 0, tiled=True)  4.15 us
    ppermute x1, starting transfers between devices, steps(): other = lax.ppermute(first[:, :, :half], 'col', swap)  2.79 us
  transfers between devices with their start and end apart: 7, of which 4 were waited for; matrix products, arithmetic and copies ran while one was open for 1% of the time, Pallas kernels for 2%

profile of v2, /device:TPU:1, one launch (start us, length us, event | category | flops | bytes accessed | tf_op | source)
XLA Modules:
  0.0 123.7 jit_solution(13663394422626276345)
XLA Ops:
  0.6 0.0 copy-start
  0.6 0.9 copy-done
  1.5 1.1 shard_map.30
  2.7 18.5 %all-to-all-start = ((bf16[128,4,1152]{2,1,0:T(4,128)(2,1)}), bf16[128,4,1152]{2,1,0:T(4,128)(2,1)S(1)}, u32[]{:S(2)}, u32[]{:S(2)}) async-start(bf16[128,4,1152]{2,1,0:T(4,128)(2,1)} %shard_map.30), calls=%async_computation | async-start | bytes 2359296 | tf_op jit(solution)/shard_map/all_to_all | solution.py:187
  21.2 0.8 shard_map.31
  22.1 33.2 %all-to-all-done = bf16[128,4,1152]{2,1,0:T(4,128)(2,1)S(1)} async-done(((bf16[128,4,1152]{2,1,0:T(4,128)(2,1)}), bf16[128,4,1152]{2,1,0:T(4,128)(2,1)S(1)}, u32[]{:S(2)}, u32[]{:S(2)}) %all-to-all-start) | async-done | bytes 1179680 | tf_op jit(solution)/shard_map/all_to_all | solution.py:187
  55.3 5.9 %all-to-all-start.1 = ((bf16[128,4,512]{2,1,0:T(4,128)(2,1)}), bf16[128,4,512]{2,1,0:T(4,128)(2,1)S(1)}, u32[]{:S(2)}, u32[]{:S(2)}) async-start(bf16[128,4,512]{2,1,0:T(4,128)(2,1)} %shard_map.31), calls=%async_computation.1 | async-start | bytes 1048576 | tf_op jit(solution)/shard_map/all_to_all | solution.py:188
  61.2 1.0 slice.4
  62.2 2.8 %collective-permute-start = (bf16[128,4,512]{2,1,0:T(4,128)(2,1)}, bf16[128,4,512]{2,1,0:T(4,128)(2,1)S(1)}, u32[]{:S(2)}, u32[]{:S(2)}) collective-permute-start(bf16[128,4,512]{2,1,0:T(4,128)(2,1)} %slice.4), channel_id=1, source_target_pairs={{0,4},{4,0},{8,12},{12,8},{16,20},{20,16},{24,28},{28,24},{1,5},{5... | collective-permute-start | bytes 1572872 | tf_op jit(solution)/shard_map/ppermute | solution.py:190
  65.0 16.5 %all-to-all-done.1 = bf16[128,4,512]{2,1,0:T(4,128)(2,1)S(1)} async-done(((bf16[128,4,512]{2,1,0:T(4,128)(2,1)}), bf16[128,4,512]{2,1,0:T(4,128)(2,1)S(1)}, u32[]{:S(2)}, u32[]{:S(2)}) %all-to-all-start.1) | async-done | bytes 524320 | tf_op jit(solution)/shard_map/all_to_all | solution.py:188
  81.5 0.1 reshape.21.right_ref
  81.6 0.3 reshape.19.own_ref
  81.9 0.1 reshape.20.other_ref
  82.1 1.6 %tile_first.1 = (bf16[512,1024]{1,0:T(8,128)(2,1)S(1)}, bf16[8,1024]{1,0:T(8,128)(2,1)S(1)}, bf16[272,640]{1,0:T(8,128)(2,1)S(1)}, bf16[272,640]{1,0:T(8,128)(2,...) custom-call(bf16[512,1152]{1,0:T(8,128)(2,1)S(1)} %reshape.19.own_ref, ...), custom_call_target="tpu_custom_call" | custom-call | flops 671088640 | bytes 2752512 | tf_op jit(solution)/shard_map/tile_first/pallas_call | solution.py:191
  83.7 0.7 copy-done.2
  84.4 2.1 %tile_second.1 = bf16[4,264,512]{2,1,0:T(8,128)(2,1)} custom-call(bf16[512,1024]{1,0:T(8,128)(2,1)S(1)} %get-tuple-element.11.left_ref, bf16[8,1024]{1,0:T(8,128)(2,1)S(1)} %get-tuple-element.12.fix_ref, bf16[512,512]{1,0:T(8,128)(2,1)S(1)} %reshape.21.right_ref), custom_call_target="tpu_custom_call" | custom-call | flops 536870912 | bytes 1572864 | tf_op jit(solution)/shard_map/tile_second/pallas_call | solution.py:218
  86.5 4.1 %all-to-all-start.2 = ((bf16[4,264,512]{2,1,0:T(8,128)(2,1)}), bf16[4,264,512]{2,1,0:T(8,128)(2,1)S(1)}, u32[]{:S(2)}, u32[]{:S(2)}) async-start(bf16[4,264,512]{2,1,0:T(8,128)(2,1)} %tile_second.1), calls=%async_computation.2 | async-start | bytes 2162688 | tf_op jit(solution)/shard_map/all_to_all | solution.py:225
  90.6 3.4 %collective-permute-start.1 = (bf16[272,640]{1,0:T(8,128)(2,1)S(1)}, bf16[272,640]{1,0:T(8,128)(2,1)S(1)}, u32[]{:S(2)}, u32[]{:S(2)}) collective-permute-start(bf16[272,640]{1,0:T(8,128)(2,1)S(1)} %copy-done.3), channel_id=1, source_target_pairs={{0,1},{1,2},{2,3},{3,0},{4,5},{5,6},{6,7},{7,4},{8,9},{9,10},{10,1... | collective-permute-start | bytes 1044488 | tf_op jit(solution)/shard_map/ppermute | solution.py:203
  94.0 4.3 %collective-permute-start.2 = (bf16[272,640]{1,0:T(8,128)(2,1)S(1)}, bf16[272,640]{1,0:T(8,128)(2,1)S(1)}, u32[]{:S(2)}, u32[]{:S(2)}) collective-permute-start(bf16[272,640]{1,0:T(8,128)(2,1)S(1)} %get-tuple-element.15), channel_id=1, source_target_pairs={{0,2},{1,3},{2,0},{3,1},{4,6},{5,7},{6,4},{7,5},{8,10},{9,11},{10,... | collective-permute-start | bytes 1044488 | tf_op jit(solution)/shard_map/ppermute | solution.py:203
  98.3 3.1 %collective-permute-start.3 = (bf16[272,640]{1,0:T(8,128)(2,1)S(1)}, bf16[272,640]{1,0:T(8,128)(2,1)S(1)}, u32[]{:S(2)}, u32[]{:S(2)}) collective-permute-start(bf16[272,640]{1,0:T(8,128)(2,1)S(1)} %get-tuple-element.16), channel_id=1, source_target_pairs={{0,3},{1,0},{2,1},{3,2},{4,7},{5,4},{6,5},{7,6},{8,11},{9,8},{10,9... | collective-permute-start | bytes 1044488 | tf_op jit(solution)/shard_map/ppermute | solution.py:203
  101.4 11.9 %collective-permute-done.1.refs_1_ = bf16[272,640]{1,0:T(8,128)(2,1)S(1)} collective-permute-done((bf16[272,640]{1,0:T(8,128)(2,1)S(1)}, bf16[272,640]{1,0:T(8,128)(2,1)S(1)}, u32[]{:S(2)}, u32[]{:S(2)}) %collective-permute-start.1) | collective-permute-done | bytes 348192 | tf_op jit(solution)/shard_map/ppermute | solution.py:203
  113.3 7.8 %collective-permute-done.2.refs_2_ = bf16[272,640]{1,0:T(8,128)(2,1)S(1)} collective-permute-done((bf16[272,640]{1,0:T(8,128)(2,1)S(1)}, bf16[272,640]{1,0:T(8,128)(2,1)S(1)}, u32[]{:S(2)}, u32[]{:S(2)}) %collective-permute-start.2) | collective-permute-done | bytes 348192 | tf_op jit(solution)/shard_map/ppermute | solution.py:203
  121.1 1.4 %join_first.1 = (f32[256,8]{1,0:T(8,128)S(1)}, f32[256,1024]{1,0:T(8,128)}, f32[256,128]{1,0:T(8,128)}) custom-call(bf16[272,640]{1,0:T(8,128)(2,1)S(1)} %get-tuple-element.13.refs_0_, bf16[272,640]{1,0:T(8,128)(2,1)S(1)} %collective-permute-done.1.refs_1_, bf16[272,640]{1,0:T(8,128)(2,1)S(1)} %collective-permute-done.2.refs_2_, ...), custom_call_target="tpu_custom_call" | custom-call | flops 1966080 | bytes 1966080 | tf_op jit(solution)/shard_map/join_first/pallas_call | solution.py:204
  122.5 1.2 join_second.1
  (8 shorter events, 0.0 us)
Async XLA Ops:
  0.6 0.9 copy-start
  2.7 18.6 %copy-start.1 = (bf16[4,16384]{1,0:T(4,128)(2,1)S(1)}, bf16[4,16384]{1,0:T(4,128)(2,1)}, u32[]{:S(2)}) copy-start(bf16[4,16384]{1,0:T(4,128)(2,1)} %x_ref.3) | copy-start | bytes 393220
  2.7 52.6 %all-to-all-start = ((bf16[128,4,1152]{2,1,0:T(4,128)(2,1)}), bf16[128,4,1152]{2,1,0:T(4,128)(2,1)S(1)}, u32[]{:S(2)}, u32[]{:S(2)}) async-start(bf16[128,4,1152]{2,1,0:T(4,128)(2,1)} %shard_map.30), calls=%async_computation | async-start | bytes 2359296 | tf_op jit(solution)/shard_map/all_to_all | solution.py:187
  55.3 26.2 %all-to-all-start.1 = ((bf16[128,4,512]{2,1,0:T(4,128)(2,1)}), bf16[128,4,512]{2,1,0:T(4,128)(2,1)S(1)}, u32[]{:S(2)}, u32[]{:S(2)}) async-start(bf16[128,4,512]{2,1,0:T(4,128)(2,1)} %shard_map.31), calls=%async_computation.1 | async-start | bytes 1048576 | tf_op jit(solution)/shard_map/all_to_all | solution.py:188
  62.2 19.7 %collective-permute-start = (bf16[128,4,512]{2,1,0:T(4,128)(2,1)}, bf16[128,4,512]{2,1,0:T(4,128)(2,1)S(1)}, u32[]{:S(2)}, u32[]{:S(2)}) collective-permute-start(bf16[128,4,512]{2,1,0:T(4,128)(2,1)} %slice.4), channel_id=1, source_target_pairs={{0,4},{4,0},{8,12},{12,8},{16,20},{20,16},{24,28},{28,24},{1,5},{5... | collective-permute-start | bytes 1572872 | tf_op jit(solution)/shard_map/ppermute | solution.py:190
  83.7 0.7 copy-start.2
  86.5 4.2 %copy-start.3 = (bf16[272,640]{1,0:T(8,128)(2,1)S(1)}, bf16[272,640]{1,0:T(8,128)(2,1)}, u32[]{:S(2)}) copy-start(bf16[272,640]{1,0:T(8,128)(2,1)} %copy-done.2) | copy-start | bytes 1044484
  86.5 36.1 %all-to-all-start.2 = ((bf16[4,264,512]{2,1,0:T(8,128)(2,1)}), bf16[4,264,512]{2,1,0:T(8,128)(2,1)S(1)}, u32[]{:S(2)}, u32[]{:S(2)}) async-start(bf16[4,264,512]{2,1,0:T(8,128)(2,1)} %tile_second.1), calls=%async_computation.2 | async-start | bytes 2162688 | tf_op jit(solution)/shard_map/all_to_all | solution.py:225
  90.6 22.7 %collective-permute-start.1 = (bf16[272,640]{1,0:T(8,128)(2,1)S(1)}, bf16[272,640]{1,0:T(8,128)(2,1)S(1)}, u32[]{:S(2)}, u32[]{:S(2)}) collective-permute-start(bf16[272,640]{1,0:T(8,128)(2,1)S(1)} %copy-done.3), channel_id=1, source_target_pairs={{0,1},{1,2},{2,3},{3,0},{4,5},{5,6},{6,7},{7,4},{8,9},{9,10},{10,1... | collective-permute-start | bytes 1044488 | tf_op jit(solution)/shard_map/ppermute | solution.py:203
  94.0 27.1 %collective-permute-start.2 = (bf16[272,640]{1,0:T(8,128)(2,1)S(1)}, bf16[272,640]{1,0:T(8,128)(2,1)S(1)}, u32[]{:S(2)}, u32[]{:S(2)}) collective-permute-start(bf16[272,640]{1,0:T(8,128)(2,1)S(1)} %get-tuple-element.15), channel_id=1, source_target_pairs={{0,2},{1,3},{2,0},{3,1},{4,6},{5,7},{6,4},{7,5},{8,10},{9,11},{10,... | collective-permute-start | bytes 1044488 | tf_op jit(solution)/shard_map/ppermute | solution.py:203
  98.3 22.8 %collective-permute-start.3 = (bf16[272,640]{1,0:T(8,128)(2,1)S(1)}, bf16[272,640]{1,0:T(8,128)(2,1)S(1)}, u32[]{:S(2)}, u32[]{:S(2)}) collective-permute-start(bf16[272,640]{1,0:T(8,128)(2,1)S(1)} %get-tuple-element.16), channel_id=1, source_target_pairs={{0,3},{1,0},{2,1},{3,2},{4,7},{5,4},{6,5},{7,6},{8,11},{9,8},{10,9... | collective-permute-start | bytes 1044488 | tf_op jit(solution)/shard_map/ppermute | solution.py:203

commit v3 on v2

v3 whole, which is shorter than its diff:
```python
import functools

import jax
import jax.numpy as jnp
from jax import lax
from jax.experimental import pallas as pl
from jax.experimental.pallas import tpu as pltpu
from jax.sharding import PartitionSpec as P


F32 = jnp.float32
BF16 = jnp.bfloat16
EPS = 1e-05


def params(mib):
    return pltpu.CompilerParams(vmem_limit_bytes=mib << 20)


def cost(flops, size):
    return pl.CostEstimate(flops=flops, bytes_accessed=size, transcendentals=0)


def thirds(v):
    hi = v.astype(BF16).astype(F32)
    rest = v - hi
    mid = rest.astype(BF16).astype(F32)
    return hi, mid, (rest - mid).astype(BF16).astype(F32)


def sums(v):
    v = v.astype(F32)
    return jnp.sum(v, axis=0, keepdims=True), jnp.sum(v * v, axis=0, keepdims=True)


def stacked(rows, count):
    gap = jnp.zeros((count - len(rows), rows[0].shape[1]), F32)
    return jnp.concatenate([*rows, gap], axis=0)


def dot0(a, b):
    return lax.dot_general(a, b, (((0,), (0,)), ((), ())), preferred_element_type=F32)


def pack_body(n_row, n_col, x_ref, out_ref):
    width = x_ref.shape[1] // n_row
    half, slab = width // 2, width // n_col
    for r in range(n_row):
        for c in range(n_col):
            d = r * n_col + c
            near = r * width + (c % 2) * half
            pair = ((r + c) % n_row) * width + (c % 2) * half
            far = ((r + n_row // 2) % n_row) * width + c * slab
            out_ref[d, :, :half] = x_ref[:, near : near + half]
            out_ref[d, :, half : 2 * half] = x_ref[:, pair : pair + half]
            out_ref[d, :, 2 * half :] = x_ref[:, far : far + slab]


def column_side(right):
    samples = right.shape[0]
    dose, square = sums(right)
    hi, mid, lo = thirds(dose)
    fix = (stacked([hi, mid, hi, mid, lo, hi], 8) * (-1.0 / samples)).astype(BF16)
    mean = dose / samples
    return fix, [*thirds(mean), *thirds(square - dose * mean)]


def tile_first(own_ref, other_ref, left_ref, fix_ref, out_ref):
    n_rep, rows, cols = out_ref.shape
    samples, half = other_ref.shape
    sub = rows - 16
    core = lax.rem(lax.axis_index("col"), 2)
    left_ref[:, pl.ds(pl.multiple_of(core * half, half), half)] = own_ref[:, :half]
    left_ref[:, pl.ds(pl.multiple_of((1 - core) * half, half), half)] = other_ref[...]
    right = own_ref[:, own_ref.shape[1] - cols :]
    right_fix, col_rows = column_side(right)
    gap = jnp.zeros((1, cols - sub), F32)
    for q in range(n_rep):
        at = slice(q * sub, (q + 1) * sub)
        left = left_ref[:, at]
        dose, square = sums(left)
        hi, mid, lo = thirds(dose)
        left_fix = stacked([hi, hi, mid, mid, hi, lo], 8).astype(BF16)
        fix_ref[:, at] = left_fix
        mean = dose / samples
        rows_of = [*thirds(mean), *thirds(square - dose * mean)]
        rows_of = [jnp.concatenate([v, gap], axis=1) for v in rows_of]
        part = dot0(left, right) + dot0(left_fix, right_fix)
        out_ref[q, :sub, :] = part.astype(BF16)
        out_ref[q, sub:, :] = stacked(col_rows + rows_of, 16).astype(BF16)


def more_tiles(left_ref, fix_ref, right, out_ref):
    n_rep, rows, _ = out_ref.shape
    sub, cols = rows - 8, right.shape[1]
    right_fix, col_rows = column_side(right)
    foot = stacked(col_rows, 8).astype(BF16)
    for q in range(n_rep):
        at = slice(q * sub, (q + 1) * sub)
        part = dot0(left_ref[:, at], right) + dot0(fix_ref[:, at], right_fix)
        out_ref[q, :sub, :cols] = part.astype(BF16)
        out_ref[q, sub:, :cols] = foot


def tile_second(first_col, left_ref, fix_ref, own_ref, out_ref):
    more_tiles(left_ref, fix_ref, own_ref[:, first_col : first_col + out_ref.shape[2]], out_ref)


def tile_third(left_ref, fix_ref, swapped_ref, second_ref, out_ref):
    cols = swapped_ref.shape[1]
    out_ref[:, :, cols:] = second_ref[...]
    more_tiles(left_ref, fix_ref, swapped_ref[...], out_ref)


def whole(means, squares, samples):
    count = len(means)
    mean = sum(means) / count
    off = [m - mean for m in means]
    spread = sum(squares) / (count * samples) + sum(o * o for o in off) / count
    return off, lax.rsqrt(spread + EPS)


def three(s, i):
    return s[i : i + 1] + s[i + 1 : i + 2] + s[i + 2 : i + 3]


def joined(parts, stats, turned, samples):
    n_rep = len(parts)
    off, scale = whole([three(s, 0) for s in stats], [three(s, 3) for s in stats], samples)
    total = sum(p.astype(F32) for p in parts)
    for q in range(n_rep):
        total += (turned[:, q : q + 1] * samples) * off[q]
    return total * turned[:, n_rep : n_rep + 1] * scale


def join_first(samples, in_ref, turned_ref, near_ref, half_ref):
    n_rep, _, _ = in_ref.shape
    sub, near = near_ref.shape
    stats = [in_ref[q, sub:, :].astype(F32) for q in range(n_rep)]
    l_off, l_scale = whole(
        [three(s[:, :sub], 6) for s in stats], [three(s[:, :sub], 9) for s in stats], samples
    )
    turned = stacked(l_off + [l_scale / (n_rep * samples)], 8).T
    total = joined([in_ref[q, :sub, :] for q in range(n_rep)], stats, turned, samples)
    near_ref[...] = total[:, :near]
    half_ref[...] = total[:, near:]
    turned_ref[...] = turned


def join_second(samples, in_ref, turned_ref, near_ref, main_ref):
    n_rep, _, _ = in_ref.shape
    sub, width = main_ref.shape
    half, near = width // 2, near_ref.shape[1]
    core = lax.rem(lax.axis_index("col"), 2)
    stats = [in_ref[q, sub:, :].astype(F32) for q in range(n_rep)]
    total = joined([in_ref[q, :sub, :] for q in range(n_rep)], stats, turned_ref[...], samples)
    mine = pl.multiple_of(core * half, half)
    main_ref[:, pl.ds(pl.multiple_of((1 - core) * half, half), half)] = total[:, :half]
    main_ref[:, pl.ds(mine, half - near)] = total[:, half:]
    main_ref[:, pl.ds(pl.multiple_of(mine + half - near, 128), near)] = near_ref[...]


def steps(genotypes):
    sample_rows, variants = genotypes.shape
    n_row, n_col, n_rep = (lax.axis_size(a) for a in ("row", "col", "rep"))
    width = variants // n_row
    half, slab = width // 2, width // n_col
    pairs = n_row * n_col
    samples = sample_rows * pairs
    sub = width // n_rep
    cols = half + slab
    near = half // 2
    one, two = near + slab, width - near
    shape = jax.ShapeDtypeStruct

    payload = pl.pallas_call(
        functools.partial(pack_body, n_row, n_col),
        out_shape=shape((pairs, sample_rows, half + cols), BF16),
        compiler_params=params(8),
        cost_estimate=cost(0, 4 * pairs * sample_rows * (half + cols)),
        name="pack",
    )(genotypes)
    arrived = lax.all_to_all(payload, ("row", "col"), 0, 0, tiled=True)

    def mate(r, c):
        return ((r - 1) % n_row) * n_col + c + 1 if c % 2 == 0 else ((r + 1) % n_row) * n_col + c - 1

    mates = [(r * n_col + c, mate(r, c)) for r in range(n_row) for c in range(n_col)]
    swapped = lax.ppermute(arrived[:, :, half : 2 * half], ("row", "col"), mates)
    other = lax.ppermute(arrived[:, :, :half], "col", [(c, c ^ 1) for c in range(n_col)])
    own = arrived.reshape(samples, half + cols)
    left, fix, part_one = pl.pallas_call(
        tile_first,
        out_shape=(
            shape((samples, width), BF16),
            shape((8, width), BF16),
            shape((n_rep, sub + 16, one), BF16),
        ),
        compiler_params=params(16),
        cost_estimate=cost(2 * samples * width * one, 2 * samples * (2 * width + one)),
        name="tile_first",
    )(own, other.reshape(samples, half))
    got_one = lax.all_to_all(part_one, "rep", 0, 0, tiled=True)
    part_two = pl.pallas_call(
        functools.partial(tile_second, half),
        out_shape=shape((n_rep, sub + 8, half - near), BF16),
        compiler_params=params(16),
        cost_estimate=cost(2 * samples * width * (half - near), 2 * samples * 2 * width),
        name="tile_second",
    )(left, fix, own)
    part_two = pl.pallas_call(
        tile_third,
        out_shape=shape((n_rep, sub + 8, two), BF16),
        compiler_params=params(16),
        cost_estimate=cost(2 * samples * width * half, 2 * samples * (width + half)),
        name="tile_third",
    )(left, fix, swapped.reshape(samples, half), part_two)
    got_two = lax.all_to_all(part_two, "rep", 0, 0, tiled=True)
    turned, near_main, far = pl.pallas_call(
        functools.partial(join_first, samples),
        out_shape=(shape((sub, 8), F32), shape((sub, near), F32), shape((sub, slab), F32)),
        compiler_params=params(8),
        cost_estimate=cost(12 * sub * one, 12 * sub * one),
        name="join_first",
    )(got_one)
    main = pl.pallas_call(
        functools.partial(join_second, samples),
        out_shape=shape((sub, width), F32),
        compiler_params=params(8),
        cost_estimate=cost(12 * sub * two, 12 * sub * two),
        name="join_second",
    )(got_two, turned, near_main)
    return main.reshape(1, 1, sub, width), far.reshape(1, sub, slab)


def solution(mesh):
    return jax.shard_map(
        steps,
        mesh=mesh,
        in_specs=(P(("row", "col", "rep"), None),),
        out_specs=(P("row", "col", "rep", None), P("row", "rep", "col")),
        check_vma=False,
    )
```

time: 124 us -> 114 us (0.919)
  blocking collectives: 0 us -> 52.3 us
  waiting for transfers between devices: 69.4 us -> 34.2 us
  starting transfers between devices: 42.1 us -> 12.9 us
  local copies, waits for them, and re-layouts: 3.16 us -> 5.88 us
    all_to_all x0 -> x1, blocking collectives: none -> 52.3 us  [steps(): arrived = lax.all_to_all(payload, ('row', 'col'), 0, 0, tiled=True)]
    all_to_all x3 -> x2, waiting for transfers between devices: 49.7 us -> 18.6 us  [the longest x1 18.6 us: steps(): got_two = lax.all_to_all(part_two, 'rep', 0, 0, tiled=True)]
    all_to_all x3 -> x2, starting transfers between devices: 28.6 us -> 8.29 us  [the longest x1 4.28 us: steps(): got_two = lax.all_to_all(part_two, 'rep', 0, 0, tiled=True)]
    ppermute x4 -> x2, starting transfers between devices: 13.5 us -> 4.62 us  [the longest x1 2.72 us: steps(): swapped = lax.ppermute(arrived[:, :, half:2 * half], ('row', 'col'), mates)]
    ppermute x4 -> x2, waiting for transfers between devices: 19.7 us -> 15.6 us  [the longest x1 13.8 us: steps(): swapped = lax.ppermute(arrived[:, :, half:2 * half], ('row', 'col'), mates)]
    reshape x2, local copies, waits for them, and re-layouts: 0.43 us -> 2.26 us  [the longest x1 1.95 us: steps(): swapped.reshape(samples, half)]
  transfers between devices with their start and end apart: 7 -> 4, of which waited for: 4 -> 3; matrix products, arithmetic and copies ran while one was open for 1% -> 2% of each run, Pallas kernels for 2% -> 4%
where the time goes in v3:
time: 114 us; the launch traced here: 113 us
  blocking collectives  52.3 us (46%)
  waiting for transfers between devices  34.2 us (30%)
  starting transfers between devices  12.9 us (11%)
  Pallas kernels  7.02 us (6%)
  local copies, waits for them, and re-layouts  5.88 us (5%)
    all_to_all x1, blocking collectives, steps(): arrived = lax.all_to_all(payload, ('row', 'col'), 0, 0, tiled=True)  52.3 us
    all_to_all x1, waiting for transfers between devices, steps(): got_two = lax.all_to_all(part_two, 'rep', 0, 0, tiled=True)  18.6 us
    ppermute x1, waiting for transfers between devices, steps(): swapped = lax.ppermute(arrived[:, :, half:2 * half], ('row', 'col'), mates)  13.8 us
    all_to_all x1, starting transfers between devices, steps(): got_two = lax.all_to_all(part_two, 'rep', 0, 0, tiled=True)  4.28 us
    all_to_all x1, starting transfers between devices, steps(): got_one = lax.all_to_all(part_one, 'rep', 0, 0, tiled=True)  4.01 us
    ppermute x1, starting transfers between devices, steps(): swapped = lax.ppermute(arrived[:, :, half:2 * half], ('row', 'col'), mates)  2.72 us
  transfers between devices with their start and end apart: 4, of which 3 were waited for; matrix products, arithmetic and copies ran while one was open for 2% of the time, Pallas kernels for 4%

profile of v3, /device:TPU:1, one launch (start us, length us, event | category | flops | bytes accessed | tf_op | source)
XLA Modules:
  0.0 113.0 jit_solution(16012140833520426727)
XLA Ops:
  0.6 0.0 copy-start.2
  0.6 0.9 copy-done.2
  1.5 0.1 pack.1
  1.6 52.3 %all_to_all.15 = bf16[128,4,1152]{2,1,0:T(4,128)(2,1)S(1)} all-to-all(bf16[128,4,1152]{2,1,0:T(4,128)(2,1)S(1)} %pack.1), channel_id=1, replica_groups=mesh['row'=16,'col'=8,'rep'=4] {'row','col'}, dimensions={0} | all-to-all | bytes 2359296 | tf_op jit(solution)/shard_map/all_to_all | solution.py:183
  53.9 1.3 %fusion = (bf16[128,4,512]{2,1,0:T(4,128)(2,1)}, bf16[128,4,512]{2,1,0:T(4,128)(2,1)}) fusion(bf16[128,4,1152]{2,1,0:T(4,128)(2,1)S(1)} %all_to_all.15), kind=kLoop, calls=%fused_computation | loop fusion | bytes 2097152 | tf_op jit(solution)/shard_map/slice | solution.py:189
  55.3 1.9 %collective-permute-start = (bf16[128,4,512]{2,1,0:T(4,128)(2,1)}, bf16[128,4,512]{2,1,0:T(4,128)(2,1)S(1)}, u32[]{:S(2)}, u32[]{:S(2)}) collective-permute-start(bf16[128,4,512]{2,1,0:T(4,128)(2,1)} %get-tuple-element.15), channel_id=1, source_target_pairs={{0,4},{4,0},{8,12},{12,8},{16,20},{20,16},{24,28},{28,24},{1,5},{5... | collective-permute-start | bytes 1572872 | tf_op jit(solution)/shard_map/ppermute | solution.py:190
  57.2 0.3 reshape.19.own_ref
  57.5 1.8 %collective-permute-done = bf16[128,4,512]{2,1,0:T(4,128)(2,1)S(1)} collective-permute-done((bf16[128,4,512]{2,1,0:T(4,128)(2,1)}, bf16[128,4,512]{2,1,0:T(4,128)(2,1)S(1)}, u32[]{:S(2)}, u32[]{:S(2)}) %collective-permute-start) | collective-permute-done | bytes 524320 | tf_op jit(solution)/shard_map/ppermute | solution.py:190
  59.3 0.1 reshape.20.other_ref
  59.4 1.3 %tile_first.1 = (bf16[512,1024]{1,0:T(8,128)(2,1)S(1)}, bf16[8,1024]{1,0:T(8,128)(2,1)S(1)}, bf16[4,272,384]{2,1,0:T(8,128)(2,1)S(1)}) custom-call(bf16[512,1152]{1,0:T(8,128)(2,1)S(1)} %reshape.19.own_ref, bf16[512,512]{1,0:T(8,128)(2,1)S(1)} %reshape.20.other_ref), custom_call_target="tpu_custom_call" | custom-call | flops 402653184 | bytes 2490368 | tf_op jit(solution)/shard_map/tile_first/pallas_call | solution.py:192
  60.7 0.0 copy-start.1
  60.7 0.9 copy-done.1
  61.6 4.0 %all-to-all-start.2 = ((bf16[4,272,384]{2,1,0:T(8,128)(2,1)}), bf16[4,272,384]{2,1,0:T(8,128)(2,1)S(1)}, u32[]{:S(2)}, u32[]{:S(2)}) async-start(bf16[4,272,384]{2,1,0:T(8,128)(2,1)} %copy-done.1), calls=%async_computation.2 | async-start | bytes 1671168 | tf_op jit(solution)/shard_map/all_to_all | solution.py:203
  65.6 2.7 %collective-permute-start.1 = (bf16[128,4,512]{2,1,0:T(4,128)(2,1)}, bf16[128,4,512]{2,1,0:T(4,128)(2,1)}, u32[]{:S(2)}, u32[]{:S(2)}) collective-permute-start(bf16[128,4,512]{2,1,0:T(4,128)(2,1)} %get-tuple-element.14), channel_id=1, source_target_pairs={{0,484},{4,32},{8,492},{12,40},{16,500},{20,48},{24,508},{28,56},{... | collective-permute-start | bytes 1572872 | tf_op jit(solution)/shard_map/ppermute | solution.py:189
  68.4 13.8 %collective-permute-done.1 = bf16[128,4,512]{2,1,0:T(4,128)(2,1)} collective-permute-done((bf16[128,4,512]{2,1,0:T(4,128)(2,1)}, bf16[128,4,512]{2,1,0:T(4,128)(2,1)}, u32[]{:S(2)}, u32[]{:S(2)}) %collective-permute-start.1) | collective-permute-done | bytes 524320 | tf_op jit(solution)/shard_map/ppermute | solution.py:189
  82.2 1.9 %reshape.21.swapped_ref = bf16[512,512]{1,0:T(8,128)(2,1)} reshape(bf16[128,4,512]{2,1,0:T(4,128)(2,1)} %collective-permute-done.1) | data formatting | bytes 1048576 | tf_op jit(solution)/shard_map/reshape | solution.py:217
  84.1 0.6 tile_second.1.second_ref
  84.8 0.4 copy-done
  85.2 2.3 %tile_third.1 = bf16[4,264,768]{2,1,0:T(8,128)(2,1)} custom-call(bf16[512,1024]{1,0:T(8,128)(2,1)S(1)} %get-tuple-element.8.left_ref, bf16[8,1024]{1,0:T(8,128)(2,1)S(1)} %get-tuple-element.9.fix_ref, bf16[512,512]{1,0:T(8,128)(2,1)S(1)} %copy-done, bf16[4,264,256]{2,1,0:T(8,128)(2,1)S(1)} %tile_second.1.second_ref), custom_call_target="tpu_custom_call" | custom-call | flops 536870912 | bytes 1572864 | tf_op jit(solution)/shard_map/tile_third/pallas_call | solution.py:211
  87.5 0.0 all-to-all-done.2.in_ref
  87.5 4.3 %all-to-all-start.1 = ((bf16[4,264,768]{2,1,0:T(8,128)(2,1)}), bf16[4,264,768]{2,1,0:T(8,128)(2,1)S(1)}, u32[]{:S(2)}, u32[]{:S(2)}) async-start(bf16[4,264,768]{2,1,0:T(8,128)(2,1)} %tile_third.1), calls=%async_computation.1 | async-start | bytes 3244032 | tf_op jit(solution)/shard_map/all_to_all | solution.py:218
  91.7 1.1 join_first.1
  92.9 18.6 %all-to-all-done.1.in_ref = bf16[4,264,768]{2,1,0:T(8,128)(2,1)S(1)} async-done(((bf16[4,264,768]{2,1,0:T(8,128)(2,1)}), bf16[4,264,768]{2,1,0:T(8,128)(2,1)S(1)}, u32[]{:S(2)}, u32[]{:S(2)}) %all-to-all-start.1) | async-done | bytes 1622048 | tf_op jit(solution)/shard_map/all_to_all | solution.py:218
  111.5 1.6 %join_second.1 = f32[256,1024]{1,0:T(8,128)} custom-call(bf16[4,264,768]{2,1,0:T(8,128)(2,1)S(1)} %all-to-all-done.1.in_ref, f32[256,8]{1,0:T(8,128)S(1)} %get-tuple-element.11.turned_ref, f32[256,256]{1,0:T(8,128)S(1)} %get-tuple-element.12.near_ref), custom_call_target="tpu_custom_call" | custom-call | flops 2359296 | bytes 2359296 | tf_op jit(solution)/shard_map/join_second/pallas_call | solution.py:226
  (1 shorter events, 0.0 us)
Async XLA Ops:
  0.6 0.9 copy-start.2
  55.3 4.0 %collective-permute-start = (bf16[128,4,512]{2,1,0:T(4,128)(2,1)}, bf16[128,4,512]{2,1,0:T(4,128)(2,1)S(1)}, u32[]{:S(2)}, u32[]{:S(2)}) collective-permute-start(bf16[128,4,512]{2,1,0:T(4,128)(2,1)} %get-tuple-element.15), channel_id=1, source_target_pairs={{0,4},{4,0},{8,12},{12,8},{16,20},{20,16},{24,28},{28,24},{1,5},{5... | collective-permute-start | bytes 1572872 | tf_op jit(solution)/shard_map/ppermute | solution.py:190
  60.7 0.9 copy-start.1
  61.6 25.8 %all-to-all-start.2 = ((bf16[4,272,384]{2,1,0:T(8,128)(2,1)}), bf16[4,272,384]{2,1,0:T(8,128)(2,1)S(1)}, u32[]{:S(2)}, u32[]{:S(2)}) async-start(bf16[4,272,384]{2,1,0:T(8,128)(2,1)} %copy-done.1), calls=%async_computation.2 | async-start | bytes 1671168 | tf_op jit(solution)/shard_map/all_to_all | solution.py:203
  65.6 16.6 %collective-permute-start.1 = (bf16[128,4,512]{2,1,0:T(4,128)(2,1)}, bf16[128,4,512]{2,1,0:T(4,128)(2,1)}, u32[]{:S(2)}, u32[]{:S(2)}) collective-permute-start(bf16[128,4,512]{2,1,0:T(4,128)(2,1)} %get-tuple-element.14), channel_id=1, source_target_pairs={{0,484},{4,32},{8,492},{12,40},{16,500},{20,48},{24,508},{28,56},{... | collective-permute-start | bytes 1572872 | tf_op jit(solution)/shard_map/ppermute | solution.py:189
  84.1 1.0 copy-start
  87.5 24.0 %all-to-all-start.1 = ((bf16[4,264,768]{2,1,0:T(8,128)(2,1)}), bf16[4,264,768]{2,1,0:T(8,128)(2,1)S(1)}, u32[]{:S(2)}, u32[]{:S(2)}) async-start(bf16[4,264,768]{2,1,0:T(8,128)(2,1)} %tile_third.1), calls=%async_computation.1 | async-start | bytes 3244032 | tf_op jit(solution)/shard_map/all_to_all | solution.py:218
